TPU v7x, 32 devices: a whole 2x2x4 slice. The times are simulated.
32 devices in a mesh: dp: 4 (over z), row: 4 (over x, core), col: 2 (over y).
Axes of the slice: x: 2, y: 2, z: 4, core: 2. Of those that a mesh axis runs over, the one named last changes fastest.
Arguments:
- block_input: float32 [23328, 1152], P(('dp', 'row'), 'col'), may hold values from -32 to 32
- qkv_weight: bfloat16 [3, 1152, 1152], P(None, 'col', 'row'), may hold values from -0.1875 to 0.1875
- query_bias: float32 [1152], P('row'), may hold values from -3 to 3
- value_bias: float32 [1152], P('row'), may hold values from -3 to 3
- out_weight: bfloat16 [1152, 1152], P('row', 'col'), may hold values from -0.75 to 0.75
- out_bias: float32 [1152], P('col'), may hold values from -2 to 2
- first_gain: float32 [1152], P('col'), may hold values from 0.3 to 2.4
- first_shift: float32 [1152], P('col'), may hold values from -2 to 2
- second_gain: float32 [1152], P('col'), may hold values from 0.3 to 2.4
- second_shift: float32 [1152], P('col'), may hold values from -2 to 2
- up_weight: bfloat16 [1152, 4304], P('col', 'row'), may hold values from -0.1875 to 0.1875
- up_bias: float32 [4304], P('row'), may hold values from -3 to 3
- down_weight: bfloat16 [4304, 1152], P('row', 'col'), may hold values from -0.09375 to 0.09375
- down_bias: float32 [1152], P('col'), may hold values from -3 to 3
- out_cotangent: float32 [23328, 1152], P(('dp', 'row'), 'col'), may hold values from -6 to 6
Outputs:
- block_output: float32 [23328, 1152], P(('dp', 'row'), 'col')
- input_grad: float32 [23328, 1152], P(('dp', 'row'), 'col')
- qkv_grad: float32 [3, 1152, 1152], P(None, 'col', 'row')
- query_bias_grad: float32 [1152], P('row')
- value_bias_grad: float32 [1152], P('row')
- out_weight_grad: float32 [1152, 1152], P('row', 'col')
- out_bias_grad: float32 [1152], P('col')
- first_gain_grad: float32 [1152], P('col')
- first_shift_grad: float32 [1152], P('col')
- second_gain_grad: float32 [1152], P('col')
- second_shift_grad: float32 [1152], P('col')
- up_weight_grad: float32 [1152, 4304], P('col', 'row')
- up_bias_grad: float32 [4304], P('row')
- down_weight_grad: float32 [4304, 1152], P('row', 'col')
- down_bias_grad: float32 [1152], P('col')
All inputs are finite; a program needn't handle non-finite values.
Results may differ from a plain program's by a relative error of at most 0.03.
Values may be sent and summed in bfloat16 or wider, within the bound.
No kernel may reach another device: no remote copies, remote signals or barrier semaphores. Data moves between devices by JAX's collectives and lax.ppermute only.
A program may use at most 320 MiB of HBM per device.

v0:
```python
import jax
import jax.numpy as jnp
from jax import lax
from jax.sharding import PartitionSpec as P

HD = 72
S = 729
IMG_DEV = 8
EPSILON = 1e-06


def gelu_tanh(tensor):
    return jax.nn.gelu(tensor, approximate=True)


def times_weight(weight_block):

    def apply_rows(row_block):
        return jnp.dot(row_block, weight_block, preferred_element_type=jnp.float32)

    return apply_rows


def times_transpose(weight_block):

    def apply_rows(row_block):
        return lax.dot_general(
            row_block, weight_block, (((1,), (1,)), ((), ())), preferred_element_type=jnp.float32
        )

    return apply_rows


def contract_rows(left, right):
    return lax.dot_general(
        left, right, (((0,), (0,)), ((), ())), preferred_element_type=jnp.float32
    )


def local_norm(values, norm_gain, norm_shift):
    width = values.shape[1] * lax.axis_size("col")
    totals, squares = lax.psum((jnp.sum(values, axis=1), jnp.sum(values * values, axis=1)), "col")
    mean_val = totals / width
    var_val = squares / width - mean_val * mean_val
    centered = values - mean_val[:, None]
    inv_dev = lax.rsqrt(var_val + EPSILON)[:, None]
    normed = centered * inv_dev
    return ((normed * norm_gain + norm_shift).astype(jnp.bfloat16), normed, inv_dev)


def local_norm_back(grad_out, normed, inv_dev, norm_gain):
    width = grad_out.shape[1] * lax.axis_size("col")
    scaled = grad_out * norm_gain
    first_sum, second_sum = lax.psum(
        (jnp.sum(scaled, axis=1), jnp.sum(scaled * normed, axis=1)), "col"
    )
    return inv_dev * (scaled - first_sum[:, None] / width - normed * (second_sum[:, None] / width))


def rows_then_width(local_rows, weight_fn):
    gathered = lax.all_gather(local_rows, "row", axis=0, tiled=True)
    return (
        gathered,
        lax.psum_scatter(
            weight_fn(gathered).astype(jnp.bfloat16), "col", scatter_dimension=0, tiled=True
        ).astype(jnp.float32),
    )


def halves_then_heads(local_rows, weight_fn):
    gathered = lax.all_gather(local_rows, "col", axis=0, tiled=True)
    return (
        gathered,
        lax.psum_scatter(
            weight_fn(gathered).astype(jnp.bfloat16), "row", scatter_dimension=0, tiled=True
        ).astype(jnp.float32),
    )


def attend_local(query_rows, key_rows, value_rows):
    score_scale = HD ** (-0.5)

    def one_image(operands):
        query_img, key_img, value_img = operands
        scores = (
            jnp.einsum("shd,thd->hst", query_img, key_img, preferred_element_type=jnp.float32)
            * score_scale
        )
        row_top = jnp.max(scores, axis=-1, keepdims=True)
        logsum = row_top + jnp.log(jnp.sum(jnp.exp(scores - row_top), axis=-1, keepdims=True))
        soft_weights = jnp.exp(scores - logsum).astype(jnp.bfloat16)
        attended = jnp.einsum(
            "hst,thd->shd", soft_weights, value_img, preferred_element_type=jnp.float32
        )
        return (attended.astype(jnp.bfloat16), logsum)

    return lax.map(one_image, (query_rows, key_rows, value_rows))


def attend_local_back(query_rows, key_rows, value_rows, logsum, grad_attended):
    score_scale = HD ** (-0.5)

    def one_image(operands):
        query_img, key_img, value_img, logsum_img, grad_img = operands
        scores = (
            jnp.einsum("shd,thd->hst", query_img, key_img, preferred_element_type=jnp.float32)
            * score_scale
        )
        soft = jnp.exp(scores - logsum_img)
        grad_value = jnp.einsum(
            "hst,shd->thd", soft.astype(jnp.bfloat16), grad_img, preferred_element_type=jnp.float32
        )
        grad_soft = jnp.einsum(
            "shd,thd->hst", grad_img, value_img, preferred_element_type=jnp.float32
        )
        row_delta = jnp.sum(soft * grad_soft, axis=-1, keepdims=True)
        grad_scores = (soft * (grad_soft - row_delta)).astype(jnp.bfloat16)
        grad_query = (
            jnp.einsum("hst,thd->shd", grad_scores, key_img, preferred_element_type=jnp.float32)
            * score_scale
        )
        grad_key = (
            jnp.einsum("hst,shd->thd", grad_scores, query_img, preferred_element_type=jnp.float32)
            * score_scale
        )
        return (
            grad_query.astype(jnp.bfloat16),
            grad_key.astype(jnp.bfloat16),
            grad_value.astype(jnp.bfloat16),
        )

    return lax.map(one_image, (query_rows, key_rows, value_rows, logsum, grad_attended))


def grid_body(
    block_input,
    qkv_weight,
    query_bias,
    value_bias,
    out_weight,
    out_bias,
    first_gain,
    first_shift,
    second_gain,
    second_shift,
    up_weight,
    up_bias,
    down_weight,
    down_bias,
    out_cotangent,
):
    images_all = IMG_DEV * lax.axis_size("dp")
    width_cols = qkv_weight.shape[1]
    head_cols = qkv_weight.shape[2]
    local_heads = head_cols // HD
    flat_qkv = jnp.transpose(qkv_weight, (1, 0, 2)).reshape(width_cols, 3 * head_cols)
    first_normed, first_hat, first_inv = local_norm(block_input, first_gain, first_shift)
    first_gathered, qkv_part = rows_then_width(first_normed, times_weight(flat_qkv))
    rows_half = qkv_part.shape[0]
    image_count = rows_half // S
    head_shape = (image_count, S, local_heads, HD)
    qkv_part = qkv_part.reshape(rows_half, 3, head_cols)
    query_rows = (qkv_part[:, 0] + query_bias).astype(jnp.bfloat16).reshape(head_shape)
    key_rows = qkv_part[:, 1].astype(jnp.bfloat16).reshape(head_shape)
    value_rows = (qkv_part[:, 2] + value_bias).astype(jnp.bfloat16).reshape(head_shape)
    attended, logsum = attend_local(query_rows, key_rows, value_rows)
    attended_flat = attended.reshape(rows_half, head_cols)
    attended_gathered, attn_proj = halves_then_heads(attended_flat, times_weight(out_weight))
    middle = block_input + attn_proj + out_bias
    second_normed, second_hat, second_inv = local_norm(middle, second_gain, second_shift)
    second_gathered, pre_act = rows_then_width(second_normed, times_weight(up_weight))
    pre_act = pre_act + up_bias
    hidden = gelu_tanh(pre_act).astype(jnp.bfloat16)
    hidden_gathered, mlp_proj = halves_then_heads(hidden, times_weight(down_weight))
    block_output = middle + mlp_proj + down_bias
    cot_rounded = out_cotangent.astype(jnp.bfloat16)
    cot_gathered, grad_hidden = rows_then_width(cot_rounded, times_transpose(down_weight))
    down_w_grad = contract_rows(hidden_gathered, cot_gathered) / images_all
    down_b_grad = jnp.sum(cot_gathered, axis=0, dtype=jnp.float32) / images_all
    grad_pre = jax.vjp(gelu_tanh, pre_act)[1](grad_hidden)[0].astype(jnp.bfloat16)
    pre_gathered, grad_second = halves_then_heads(grad_pre, times_transpose(up_weight))
    up_w_grad = contract_rows(second_gathered, pre_gathered) / images_all
    up_b_grad = jnp.sum(pre_gathered, axis=0, dtype=jnp.float32) / images_all
    second_gain_part = jnp.sum(grad_second * second_hat, axis=0) / images_all
    second_shift_part = jnp.sum(grad_second, axis=0) / images_all
    grad_middle = out_cotangent + local_norm_back(grad_second, second_hat, second_inv, second_gain)
    middle_rounded = grad_middle.astype(jnp.bfloat16)
    middle_gathered, grad_attended = rows_then_width(middle_rounded, times_transpose(out_weight))
    out_w_grad = contract_rows(attended_gathered, middle_gathered) / images_all
    out_b_grad = jnp.sum(middle_gathered, axis=0, dtype=jnp.float32) / images_all
    grad_attended = grad_attended.astype(jnp.bfloat16).reshape(head_shape)
    grad_query, grad_key, grad_value = attend_local_back(
        query_rows, key_rows, value_rows, logsum, grad_attended
    )
    grad_qkv = jnp.stack(
        [
            grad_query.reshape(rows_half, head_cols),
            grad_key.reshape(rows_half, head_cols),
            grad_value.reshape(rows_half, head_cols),
        ],
        axis=1,
    ).reshape(rows_half, 3 * head_cols)
    qkv_gathered, grad_first = halves_then_heads(grad_qkv, times_transpose(flat_qkv))
    qkv_w_grad = (
        (contract_rows(first_gathered, qkv_gathered) / images_all)
        .reshape(width_cols, 3, head_cols)
        .transpose(1, 0, 2)
    )
    query_b_grad = jnp.sum(qkv_gathered[:, :head_cols], axis=0, dtype=jnp.float32) / images_all
    value_b_grad = jnp.sum(qkv_gathered[:, 2 * head_cols :], axis=0, dtype=jnp.float32) / images_all
    (
        qkv_w_grad,
        query_b_grad,
        value_b_grad,
        out_w_grad,
        out_b_grad,
        up_w_grad,
        up_b_grad,
        down_w_grad,
        down_b_grad,
    ) = (
        lax.psum(qkv_w_grad.astype(jnp.bfloat16), "dp").astype(jnp.float32),
        lax.psum(query_b_grad.astype(jnp.bfloat16), "dp").astype(jnp.float32),
        lax.psum(value_b_grad.astype(jnp.bfloat16), "dp").astype(jnp.float32),
        lax.psum(out_w_grad.astype(jnp.bfloat16), "dp").astype(jnp.float32),
        lax.psum(out_b_grad.astype(jnp.bfloat16), "dp").astype(jnp.float32),
        lax.psum(up_w_grad.astype(jnp.bfloat16), "dp").astype(jnp.float32),
        lax.psum(up_b_grad.astype(jnp.bfloat16), "dp").astype(jnp.float32),
        lax.psum(down_w_grad.astype(jnp.bfloat16), "dp").astype(jnp.float32),
        lax.psum(down_b_grad.astype(jnp.bfloat16), "dp").astype(jnp.float32),
    )
    first_gain_part = jnp.sum(grad_first * first_hat, axis=0) / images_all
    first_shift_part = jnp.sum(grad_first, axis=0) / images_all
    grad_input = grad_middle + local_norm_back(grad_first, first_hat, first_inv, first_gain)
    first_gain_grad, first_shift_grad, second_gain_grad, second_shift_grad = lax.psum(
        (first_gain_part, first_shift_part, second_gain_part, second_shift_part), ("dp", "row")
    )
    return (
        block_output,
        grad_input,
        qkv_w_grad,
        query_b_grad,
        value_b_grad,
        out_w_grad,
        out_b_grad,
        first_gain_grad,
        first_shift_grad,
        second_gain_grad,
        second_shift_grad,
        up_w_grad,
        up_b_grad,
        down_w_grad,
        down_b_grad,
    )


def shards(
    block_input,
    qkv_weight,
    query_bias,
    value_bias,
    out_weight,
    out_bias,
    first_gain,
    first_shift,
    second_gain,
    second_shift,
    up_weight,
    up_bias,
    down_weight,
    down_bias,
    out_cotangent,
):
    return grid_body(
        block_input,
        qkv_weight,
        query_bias,
        value_bias,
        out_weight,
        out_bias,
        first_gain,
        first_shift,
        second_gain,
        second_shift,
        up_weight,
        up_bias,
        down_weight,
        down_bias,
        out_cotangent,
    )


def solution(mesh):
    return jax.shard_map(
        shards,
        mesh=mesh,
        in_specs=(
            P(("dp", "row"), "col"),
            P(None, "col", "row"),
            P("row"),
            P("row"),
            P("row", "col"),
            P("col"),
            P("col"),
            P("col"),
            P("col"),
            P("col"),
            P("col", "row"),
            P("row"),
            P("row", "col"),
            P("col"),
            P(("dp", "row"), "col"),
        ),
        out_specs=(
            P(("dp", "row"), "col"),
            P(("dp", "row"), "col"),
            P(None, "col", "row"),
            P("row"),
            P("row"),
            P("row", "col"),
            P("col"),
            P("col"),
            P("col"),
            P("col"),
            P("col"),
            P("col", "row"),
            P("row"),
            P("row", "col"),
            P("col"),
        ),
        check_vma=False,
    )
```

profile of v0, /device:TPU:0, one launch (start us, length us, event | category | flops | bytes accessed | tf_op | source)
XLA Modules:
  0.0 2734.9 jit_solution(11299218937479715153)
XLA Ops:
  24.0 51.2 %all-gather.17.cloned.1.call-done = bf16[4,1458,576]{1,2,0:T(8,128)(2,1)} async-done(((bf16[1,1458,576]{1,2,0:T(8,128)(2,1)}), bf16[4,1458,576]{1,2,0:T(8,128)(2,1)}) %all-gather.17.cloned.1.call-update) | async-done | bytes 6718480 | tf_op jit(solution)/shard_map/all_gather | solution.py:61
  114.4 234.6 %all-reduce.25.cloned.1.call-done = bf16[5832,864]{0,1:T(8,128)(2,1)} async-done(((bf16[5832,864]{0,1:T(8,128)(2,1)}), bf16[5832,864]{0,1:T(8,128)(2,1)}) %all-reduce.25.cloned.1.call-update) | async-done | bytes 10077712
  384.8 29.9 %while.26 = (s32[]{:T(128)}, bf16[4,729,4,72]{1,3,2,0:T(8,128)(2,1)}, f32[4,4,729,1]{2,1,3,0:T(4,128)S(1)}, bf16[4,729,4,72]{1,3,2,0:T(8,128)(2,1)}, bf16[4,729,...) while((s32[]{:T(128)}, bf16[4,729,4,72]{1,3,2,0:T(8,128)(2,1)}, ...), condition=%wide.region_8.9_spmd, body=%wide.region_5.8_spmd.sunk | while | flops 629433152 | bytes 27376584 | solution.py:97
  434.2 47.8 %all-gather.19.cloned.1.call-done = bf16[2,2916,288]{1,2,0:T(8,128)(2,1)} async-done(((bf16[1,2916,288]{1,2,0:T(8,128)(2,1)}), bf16[2,2916,288]{1,2,0:T(8,128)(2,1)}) %all-gather.19.cloned.1.call-update) | async-done | bytes 3359248 | tf_op jit(solution)/shard_map/all_gather | solution.py:71
  508.0 122.8 %all-reduce.27.cloned.1.call-done = bf16[5832,576]{0,1:T(8,128)(2,1)} async-done(((bf16[5832,576]{0,1:T(8,128)(2,1)}), bf16[5832,576]{0,1:T(8,128)(2,1)}) %all-reduce.27.cloned.1.call-update) | async-done | bytes 6718480
  648.5 34.8 %all-gather.25.cloned.1.call-done = bf16[4,1458,576]{1,2,0:T(8,128)(2,1)} async-done(((bf16[1,1458,576]{1,2,0:T(8,128)(2,1)}), bf16[4,1458,576]{1,2,0:T(8,128)(2,1)}) %all-gather.25.cloned.1.call-update) | async-done | bytes 6718480 | tf_op jit(solution)/shard_map/all_gather | solution.py:61
  708.5 15.8 convolution_convert_fusion
  760.2 16.1 convolution_convert_fusion.1
  776.3 563.8 %all-reduce.37.cloned.1.call-done = (bf16[5832,1076]{0,1:T(8,128)(2,1)}, bf16[5832,1076]{0,1:T(8,128)(2,1)}) async-done(((bf16[5832,1076]{0,1:T(8,128)(2,1)}, bf16[5832,1076]{0,1:T(8,128)(2,1)}), (bf16[5832,1076]{0,1:T(8,128)(2,1)}, bf16[5832,1076]{0,1:T(8,128)(2,1)})) %all-reduce.37.cloned.1.call-update) | async-done | bytes 25100944
  1340.1 20.3 fusion.71
  1360.5 154.6 %all-gather.27.cloned.1.call-done = bf16[2,2916,1076]{1,2,0:T(8,128)(2,1)} async-done(((bf16[1,2916,1076]{1,2,0:T(8,128)(2,1)}), bf16[2,2916,1076]{1,2,0:T(8,128)(2,1)}) %all-gather.27.cloned.1.call-update) | async-done | bytes 12550480 | tf_op jit(solution)/shard_map/all_gather | solution.py:71
  1515.1 48.6 %copy.73 = bf16[2,2916,1076]{1,0,2:T(2,128)(2,1)} copy(bf16[2,2916,1076]{1,2,0:T(8,128)(2,1)} %all-gather.27.cloned.1.call-done) | data formatting | bytes 25100928 | tf_op jit(solution)/shard_map/all_gather | solution.py:71
  1563.7 25.6 reshape.132
  1604.7 127.7 %all-reduce.29.cloned.1.call-done = bf16[5832,576]{0,1:T(8,128)(2,1)} async-done(((bf16[5832,576]{0,1:T(8,128)(2,1)}), bf16[5832,576]{0,1:T(8,128)(2,1)}) %all-reduce.29.cloned.1.call-update) | async-done | bytes 6718480
  1753.2 49.8 %all-gather.29.cloned.1.call-done = bf16[4,1458,576]{1,2,0:T(8,128)(2,1)} async-done(((bf16[1,1458,576]{1,2,0:T(8,128)(2,1)}), bf16[4,1458,576]{1,2,0:T(8,128)(2,1)}) %all-gather.29.cloned.1.call-update) | async-done | bytes 6718480 | tf_op jit(solution)/shard_map/all_gather | solution.py:61
  1834.9 90.5 %all-reduce.31.cloned.1.call-done = bf16[5832,288]{0,1:T(8,128)(2,1)} async-done(((bf16[5832,288]{0,1:T(8,128)(2,1)}), bf16[5832,288]{0,1:T(8,128)(2,1)}) %all-reduce.31.cloned.1.call-update) | async-done | bytes 3359248
  1941.6 118.4 %while.27 = (s32[]{:T(128)}, bf16[4,729,4,72]{1,3,2,0:T(8,128)(2,1)}, bf16[4,729,4,72]{1,3,2,0:T(8,128)(2,1)}, bf16[4,729,4,72]{1,3,2,0:T(8,128)(2,1)}, bf16[4,7...) while((s32[]{:T(128)}, ...), condition=%wide.region_25.26_spmd, body=%wide.region_23.25_spmd.sunk | while | flops 1557106048 | bytes 127373888 | solution.py:132
  2086.5 48.3 %copy.71 = bf16[2,2916,1076]{1,0,2:T(2,128)(2,1)} copy(bf16[2,2916,1076]{1,2,0:T(8,128)(2,1)} %all-gather.23.cloned.1.call-done) | data formatting | bytes 25100928 | tf_op jit(solution)/shard_map/all_gather | solution.py:71
  2134.8 25.6 reshape.128
  2193.5 19.3 all-gather.31.cloned.1.call-done
  2303.8 20.4 all-reduce.14
  2327.1 80.7 %all-reduce.35.cloned.1.call-done = (bf16[3,576,288]{1,2,0:T(8,128)(2,1)}, bf16[288,576]{1,0:T(8,128)(2,1)}, bf16[576,1076]{1,0:T(8,128)(2,1)}, bf16[1076,576]{0,1:T(8,128)(2,1)}) async-done(((bf16[3,576,288]{1,2,0:T(8,128)(2,1)}, bf16[288,576]{1,0:T(8,128)(2,1)}, bf16[576,1076]{1,0:T(8,128)(2,1)}, bf16[1076,576]{0,1:T(8,128)(2,1)}), (bf16[3,576,288]{1,2,0:T(8,128)(2,1)}, bf16[288,576]{1,0:T(8,128)(2,1)}, ...) | async-done | bytes 3806224 | tf_op jit(solution)/shard_map/psum | solution.py:222
  2416.1 229.7 %all-reduce.33.cloned.1.call-done = (bf16[5832,576]{0,1:T(8,128)(2,1)}, bf16[5832,576]{0,1:T(8,128)(2,1)}) async-done(((bf16[5832,576]{0,1:T(8,128)(2,1)}, bf16[5832,576]{0,1:T(8,128)(2,1)}), (bf16[5832,576]{0,1:T(8,128)(2,1)}, bf16[5832,576]{0,1:T(8,128)(2,1)})) %all-reduce.33.cloned.1.call-update) | async-done | bytes 13436944
  2659.0 58.9 %all-reduce.8 = (f32[576]{0:T(1024)}, f32[576]{0:T(1024)}, f32[576]{0:T(1024)}, f32[576]{0:T(1024)}) all-reduce(f32[576]{0:T(1024)S(1)} %broadcast_multiply_fusion.9, f32[576]{0:T(1024)S(1)} %broadcast_multiply_fusion.8, f32[576]{0:T(1024)S(1)} %get-tuple-element.228, ...), channel_id=1, replica_groups=mesh['dp'=4,'row'=4,'col'=2] {'dp','row'}, use_global_device_ids=true, to_apply=%region_40.41 | all-reduce | flops 2304 | bytes 18432 | tf_op jit(solution)/shard_map/psum | solution.py:235
  (275 shorter events, 631.5 us)
Async XLA Ops:
  7.2 753.0 %copy-start = (bf16[576,1076]{1,0:T(8,128)(2,1)S(1)}, bf16[576,1076]{1,0:T(8,128)(2,1)}, u32[]{:S(2)}) copy-start(bf16[576,1076]{1,0:T(8,128)(2,1)} %param.29) | copy-start | bytes 3718660
  7.2 67.9 %all-gather.17.cloned.1.call-start = ((), (), s32[]{:S(2)}) async-start(), calls=%async_computation | async-start | bytes 8847360 | tf_op jit(solution)/shard_map/all_gather | solution.py:61
  23.9 325.1 %all-reduce.25.cloned.1.call-start = ((), (), s32[]{:S(2)}) async-start(), calls=%async_computation.8 | async-start | bytes 20348928
  112.3 369.7 %all-gather.19.cloned.1.call-start = ((), (), s32[]{:S(2)}) async-start(), calls=%async_computation.1 | async-start | bytes 5087232 | tf_op jit(solution)/shard_map/all_gather | solution.py:71
  434.1 196.7 %all-reduce.27.cloned.1.call-start = ((), (), s32[]{:S(2)}) async-start(), calls=%async_computation.9 | async-start | bytes 13565952
  503.2 180.2 %all-gather.25.cloned.1.call-start = ((), (), s32[]{:S(2)}) async-start(), calls=%async_computation.4 | async-start | bytes 8847360 | tf_op jit(solution)/shard_map/all_gather | solution.py:61
  506.7 229.5 %all-gather.21.cloned.1.call-start = ((), (), s32[]{:S(2)}) async-start(), calls=%async_computation.2 | async-start | bytes 8847360 | tf_op jit(solution)/shard_map/all_gather | solution.py:61
  644.6 1101.4 %copy-start.10 = (f32[1458]{0:T(1024)}, f32[1458]{0:T(1024)S(1)}, u32[]{:S(2)}) copy-start(f32[1458]{0:T(1024)S(1)} %get-tuple-element.223) | copy-start | bytes 17500
  644.7 1101.4 %copy-start.12 = (f32[1458]{0:T(1024)}, f32[1458]{0:T(1024)S(1)}, u32[]{:S(2)}) copy-start(f32[1458]{0:T(1024)S(1)} %get-tuple-element.224) | copy-start | bytes 17500
  648.5 691.6 %all-reduce.37.cloned.1.call-start = ((), (), s32[]{:S(2)}) async-start(), calls=%async_computation.14 | async-start | bytes 50872320
  776.2 563.9 %copy-start.28 = (f32[1076]{0:T(1024)S(1)}, f32[1076]{0:T(1024)}, u32[]{:S(2)}) copy-start(f32[1076]{0:T(1024)} %param.30) | copy-start | bytes 12916
  776.3 738.9 %all-gather.27.cloned.1.call-start = ((), (), s32[]{:S(2)}) async-start(), calls=%async_computation.5 | async-start | bytes 19077120 | tf_op jit(solution)/shard_map/all_gather | solution.py:71
  1360.5 371.8 %all-reduce.29.cloned.1.call-start = ((), (), s32[]{:S(2)}) async-start(), calls=%async_computation.10 | async-start | bytes 13565952
  1604.6 198.5 %all-gather.29.cloned.1.call-start = ((), (), s32[]{:S(2)}) async-start(), calls=%async_computation.6 | async-start | bytes 8847360 | tf_op jit(solution)/shard_map/all_gather | solution.py:61
  1752.8 172.6 %all-reduce.31.cloned.1.call-start = ((), (), s32[]{:S(2)}) async-start(), calls=%async_computation.11 | async-start | bytes 6782976
  1834.1 252.4 %all-gather.23.cloned.1.call-start = ((), (), s32[]{:S(2)}) async-start(), calls=%async_computation.3 | async-start | bytes 19077120 | tf_op jit(solution)/shard_map/all_gather | solution.py:71
  1834.7 378.1 %all-gather.31.cloned.1.call-start = ((), (), s32[]{:S(2)}) async-start(), calls=%async_computation.7 | async-start | bytes 15261696 | tf_op jit(solution)/shard_map/all_gather | solution.py:71
  2086.4 321.4 %all-reduce.35.cloned.1.call-start = ((), (), s32[]{:S(2)}) async-start(), calls=%async_computation.13 | async-start | bytes 8257536 | tf_op jit(solution)/shard_map/psum | solution.py:222
  2254.3 391.5 %all-reduce.33.cloned.1.call-start = ((), (), s32[]{:S(2)}) async-start(), calls=%async_computation.12 | async-start | bytes 27131904
  2416.1 301.7 %copy-start.13 = (f32[1458]{0:T(1024)S(1)}, f32[1458]{0:T(1024)}, u32[]{:S(2)}) copy-start(f32[1458]{0:T(1024)} %copy-done.12) | copy-start | bytes 17500
  2416.1 301.7 %copy-start.19 = (f32[1458]{0:T(1024)S(1)}, f32[1458]{0:T(1024)}, u32[]{:S(2)}) copy-start(f32[1458]{0:T(1024)} %copy-done.18) | copy-start | bytes 17500
  2416.1 301.8 %copy-start.21 = (f32[1458]{0:T(1024)S(1)}, f32[1458]{0:T(1024)}, u32[]{:S(2)}) copy-start(f32[1458]{0:T(1024)} %copy-done.20) | copy-start | bytes 17500
  2416.1 301.8 %copy-start.23 = (f32[576]{0:T(1024)S(1)}, f32[576]{0:T(1024)}, u32[]{:S(2)}) copy-start(f32[576]{0:T(1024)} %param.27) | copy-start | bytes 6916
  2416.1 301.8 %copy-start.30 = (f32[576]{0:T(1024)S(1)}, f32[576]{0:T(1024)}, u32[]{:S(2)}) copy-start(f32[576]{0:T(1024)} %param.32) | copy-start | bytes 6916
  (43 other events, 1633.5 us)
Sparse Core Ops, SparseCore 0:
  24.1 51.0 all-gather.16
  112.4 236.5 all-reduce.24
  434.3 47.6 all-gather.18
  503.3 127.5 all-reduce.26
  632.3 51.0 all-gather.24
  685.3 50.8 all-gather.20
  776.4 563.6 all-reduce.36
  1360.6 154.4 all-gather.26
  1604.7 127.5 all-reduce.28
  1752.9 50.1 all-gather.28
  1834.2 91.1 all-reduce.30
  1926.8 153.9 all-gather.22
  2086.5 126.1 all-gather.30
  2254.4 153.3 all-reduce.34
  2410.3 235.4 all-reduce.32
where the time goes:
time: 2750 us; the launch traced here: 2730 us
  waiting for transfers between devices  1820 us (66%)
  local copies, waits for them, and re-layouts  380 us (14%)
  matrix products  247 us (9%)
  other arithmetic  157 us (6%)
  blocking collectives  113 us (4%)
    unnamed x21, waiting for transfers between devices  1370 us
    all_gather x4, waiting for transfers between devices, halves_then_heads(): gathered = lax.all_gather(local_rows, 'col', axis=0, tiled=True)  222 us
    unnamed x93, local copies, waits for them, and re-layouts  149 us
    all_gather x4, waiting for transfers between devices, rows_then_width(): gathered = lax.all_gather(local_rows, 'row', axis=0, tiled=True)  148 us
    all_gather x4, local copies, waits for them, and re-layouts, halves_then_heads(): gathered = lax.all_gather(local_rows, 'col', axis=0, tiled=True)  117 us
    psum x1, waiting for transfers between devices, grid_body(): lax.psum(qkv_w_grad.astype(jnp.bfloat16), 'dp').astype(jnp.float32)  80.7 us
    psum x1, blocking collectives, grid_body(): lax.psum((first_gain_part, first_shift_part, second_gain_part, second_shi...  58.9 us
  transfers between devices with their start and end apart: 15, of which 14 were waited for; matrix products, arithmetic and copies ran while one was open for 14% of the time, Pallas kernels for 0%

commit v1 on v0

--- a/solution.py
+++ b/solution.py
@@ -7,6 +7,28 @@
 S = 729
 IMG_DEV = 8
 EPSILON = 1e-06
+
+
+def laid_out(parts, dim):
+    shape = list(parts.shape[1:])
+    shape[dim] *= parts.shape[0]
+    return jnp.moveaxis(parts, 0, dim).reshape(shape)
+
+
+def doubled(x, axis):
+    size = lax.axis_size(axis)
+    tiles = x[None]
+    for level in range(size.bit_length() - 1):
+        bit = 1 << level
+        other = lax.ppermute(tiles, axis, [(i, i ^ bit) for i in range(size)])
+        both = jnp.stack([tiles, other])
+        upper = lax.axis_index(axis) >> level & 1
+        tiles = jnp.where(upper == 0, both, both[::-1]).reshape(-1, *x.shape)
+    return tiles
+
+
+def collect(x, axis, dim):
+    return laid_out(doubled(x, axis), dim)
 
 
 def gelu_tanh(tensor):
@@ -58,7 +80,7 @@
 
 
 def rows_then_width(local_rows, weight_fn):
-    gathered = lax.all_gather(local_rows, "row", axis=0, tiled=True)
+    gathered = collect(local_rows, "row", 0)
     return (
         gathered,
         lax.psum_scatter(

time: 2750 us -> 2980 us (1.084)
  local copies, waits for them, and re-layouts: 380 us -> 473 us
  waiting for transfers between devices: 1820 us -> 1910 us
  other arithmetic: 157 us -> 200 us
    ppermute x0 -> x8, waiting for transfers between devices: none -> 174 us  [doubled(): other = lax.ppermute(tiles, axis, [(i, i ^ bit) for i in range(size)])]
    all_gather x4 -> x0, waiting for transfers between devices: 148 us -> none  [rows_then_width(): gathered = lax.all_gather(local_rows, 'row', axis=0, tiled=True)]
    select_n x0 -> x4, local copies, waits for them, and re-layouts: none -> 137 us  [doubled(): tiles = jnp.where(upper == 0, both, both[::-1]).reshape(-1, *x.shape)]
    unnamed x21 -> x17, waiting for transfers between devices: 1370 us -> 1420 us
    another operation x4 -> x8, local copies, waits for them, and re-layouts: 5.36 us -> 55.7 us  [the longest x4 50.3 us: laid_out(): return jnp.moveaxis(parts, 0, dim).reshape(shape)]
    unnamed x93 -> x97, local copies, waits for them, and re-layouts: 149 us -> 100 us
    all_gather x4 -> x0, local copies, waits for them, and re-layouts: 45.9 us -> none  [rows_then_width(): gathered = lax.all_gather(local_rows, 'row', axis=0, tiled=True)]
    another operation x0 -> x16, other arithmetic: none -> 38.9 us  [doubled(): both = jnp.stack([tiles, other])]
  transfers between devices with their start and end apart: 15 -> 19, of which waited for: 14 -> 17; matrix products, arithmetic and copies ran while one was open for 14% -> 14% of each run, Pallas kernels for 0% -> 0%
where the time goes in v1:
time: 2980 us; the launch traced here: 2960 us
  waiting for transfers between devices  1910 us (64%)
  local copies, waits for them, and re-layouts  473 us (16%)
  matrix products  248 us (8%)
  other arithmetic  200 us (7%)
  blocking collectives  113 us (4%)
    unnamed x17, waiting for transfers between devices  1420 us
    all_gather x4, waiting for transfers between devices, halves_then_heads(): gathered = lax.all_gather(local_rows, 'col', axis=0, tiled=True)  222 us
    ppermute x8, waiting for transfers between devices, doubled(): other = lax.ppermute(tiles, axis, [(i, i ^ bit) for i in range(size)])  174 us
    select_n x4, local copies, waits for them, and re-layouts, doubled(): tiles = jnp.where(upper == 0, both, both[::-1]).reshape(-1, *x.shape)  137 us
    all_gather x4, local copies, waits for them, and re-layouts, halves_then_heads(): gathered = lax.all_gather(local_rows, 'col', axis=0, tiled=True)  117 us
    unnamed x97, local copies, waits for them, and re-layouts  100 us
    psum x1, waiting for transfers between devices, grid_body(): lax.psum(qkv_w_grad.astype(jnp.bfloat16), 'dp').astype(jnp.float32)  88.2 us
  transfers between devices with their start and end apart: 19, of which 17 were waited for; matrix products, arithmetic and copies ran while one was open for 14% of the time, Pallas kernels for 0%

profile of v1, /device:TPU:0, one launch (start us, length us, event | category | flops | bytes accessed | tf_op | source)
XLA Modules:
  0.0 2962.0 jit_solution(17905666345566759515)
XLA Ops:
  32.8 77.4 %collective-permute-done.1 = bf16[2,1458,576]{1,2,0:T(8,128)(2,1)} collective-permute-done((bf16[2,1458,576]{1,2,0:T(8,128)(2,1)}, bf16[2,1458,576]{1,2,0:T(8,128)(2,1)}, u32[]{:S(2)}, u32[]{:S(2)}) %collective-permute-start.1) | collective-permute-done | bytes 3359264 | tf_op jit(solution)/shard_map/ppermute | solution.py:23
  118.2 34.2 %copy.73 = bf16[2,2,1458,576]{2,1,0,3:T(2,128)(2,1)} copy(bf16[2,2,1458,576]{2,3,1,0:T(8,128)(2,1)} %reverse_select_fusion.3) | data formatting | bytes 13436928 | tf_op jit(solution)/shard_map/jit(_where)/select_n | solution.py:26
  180.2 234.9 %all-reduce.25.cloned.1.call-done = bf16[5832,864]{0,1:T(8,128)(2,1)} async-done(((bf16[5832,864]{0,1:T(8,128)(2,1)}), bf16[5832,864]{0,1:T(8,128)(2,1)}) %all-reduce.25.cloned.1.call-update) | async-done | bytes 10077712
  451.0 32.2 %while.26 = (s32[]{:T(128)}, bf16[4,729,4,72]{1,3,2,0:T(8,128)(2,1)}, f32[4,4,729,1]{2,1,3,0:T(4,128)}, bf16[4,729,4,72]{1,3,2,0:T(8,128)(2,1)}, bf16[4,729,4,72...) while((s32[]{:T(128)}, bf16[4,729,4,72]{1,3,2,0:T(8,128)(2,1)}, ...), condition=%wide.region_8.9_spmd, body=%wide.region_5.8_spmd.sunk | while | flops 629433152 | bytes 27374712 | solution.py:119
  503.4 47.8 %all-gather.9.cloned.1.call-done = bf16[2,2916,288]{1,2,0:T(8,128)(2,1)} async-done(((bf16[1,2916,288]{1,2,0:T(8,128)(2,1)}), bf16[2,2916,288]{1,2,0:T(8,128)(2,1)}) %all-gather.9.cloned.1.call-update) | async-done | bytes 3359248 | tf_op jit(solution)/shard_map/all_gather | solution.py:93
  588.4 176.8 %all-reduce.27.cloned.1.call-done = bf16[5832,576]{0,1:T(8,128)(2,1)} async-done(((bf16[5832,576]{0,1:T(8,128)(2,1)}), bf16[5832,576]{0,1:T(8,128)(2,1)}) %all-reduce.27.cloned.1.call-update) | async-done | bytes 6718480
  798.4 34.6 %copy.83 = bf16[2,2,1458,576]{2,1,0,3:T(2,128)(2,1)} copy(bf16[2,2,1458,576]{2,3,1,0:T(8,128)(2,1)} %get-tuple-element.213) | data formatting | bytes 13436928 | tf_op jit(solution)/shard_map/jit(_where)/select_n | solution.py:26
  875.5 34.2 %copy.80 = bf16[2,2,1458,576]{2,1,0,3:T(2,128)(2,1)} copy(bf16[2,2,1458,576]{2,3,1,0:T(8,128)(2,1)} %reverse_select_fusion.2) | data formatting | bytes 13436928 | tf_op jit(solution)/shard_map/jit(_where)/select_n | solution.py:26
  938.4 562.9 %all-reduce.37.cloned.1.call-done = (bf16[5832,1076]{0,1:T(8,128)(2,1)}, bf16[5832,1076]{0,1:T(8,128)(2,1)}) async-done(((bf16[5832,1076]{0,1:T(8,128)(2,1)}, bf16[5832,1076]{0,1:T(8,128)(2,1)}), (bf16[5832,1076]{0,1:T(8,128)(2,1)}, bf16[5832,1076]{0,1:T(8,128)(2,1)})) %all-reduce.37.cloned.1.call-update) | async-done | bytes 25100944
  1501.3 20.4 fusion.71
  1521.7 154.6 %all-gather.13.cloned.1.call-done = bf16[2,2916,1076]{1,2,0:T(8,128)(2,1)} async-done(((bf16[1,2916,1076]{1,2,0:T(8,128)(2,1)}), bf16[2,2916,1076]{1,2,0:T(8,128)(2,1)}) %all-gather.13.cloned.1.call-update) | async-done | bytes 12550480 | tf_op jit(solution)/shard_map/all_gather | solution.py:93
  1676.3 48.5 %copy.84 = bf16[2,2916,1076]{1,0,2:T(2,128)(2,1)} copy(bf16[2,2916,1076]{1,2,0:T(8,128)(2,1)} %all-gather.13.cloned.1.call-done) | data formatting | bytes 25100928 | tf_op jit(solution)/shard_map/all_gather | solution.py:93
  1724.9 25.6 reshape.142
  1765.8 127.7 %all-reduce.29.cloned.1.call-done = bf16[5832,576]{0,1:T(8,128)(2,1)} async-done(((bf16[5832,576]{0,1:T(8,128)(2,1)}), bf16[5832,576]{0,1:T(8,128)(2,1)}) %all-reduce.29.cloned.1.call-update) | async-done | bytes 6718480
  1919.1 77.8 %collective-permute-done.7 = bf16[2,1458,576]{1,2,0:T(8,128)(2,1)S(1)} collective-permute-done((bf16[2,1458,576]{1,2,0:T(8,128)(2,1)S(1)}, bf16[2,1458,576]{1,2,0:T(8,128)(2,1)S(1)}, u32[]{:S(2)}, u32[]{:S(2)}) %collective-permute-start.7) | collective-permute-done | bytes 3359264 | tf_op jit(solution)/shard_map/ppermute | solution.py:23
  2006.9 34.2 %copy.86 = bf16[2,2,1458,576]{2,1,0,3:T(2,128)(2,1)} copy(bf16[2,2,1458,576]{2,3,1,0:T(8,128)(2,1)} %get-tuple-element.215) | data formatting | bytes 13436928 | tf_op jit(solution)/shard_map/jit(_where)/select_n | solution.py:26
  2061.7 89.7 %all-reduce.31.cloned.1.call-done = bf16[5832,288]{0,1:T(8,128)(2,1)} async-done(((bf16[5832,288]{0,1:T(8,128)(2,1)}), bf16[5832,288]{0,1:T(8,128)(2,1)}) %all-reduce.31.cloned.1.call-update) | async-done | bytes 3359248
  2164.8 121.4 %while.27 = (s32[]{:T(128)}, bf16[4,729,4,72]{1,3,2,0:T(8,128)(2,1)}, bf16[4,729,4,72]{1,3,2,0:T(8,128)(2,1)}, bf16[4,729,4,72]{1,3,2,0:T(8,128)(2,1)}, bf16[4,7...) while((s32[]{:T(128)}, ...), condition=%wide.region_25.26_spmd, body=%wide.region_23.25_spmd.sunk | while | flops 1557106048 | bytes 127373888 | solution.py:154
  2312.8 48.3 %copy.81 = bf16[2,2916,1076]{1,0,2:T(2,128)(2,1)} copy(bf16[2,2916,1076]{1,2,0:T(8,128)(2,1)} %all-gather.11.cloned.1.call-done) | data formatting | bytes 25100928 | tf_op jit(solution)/shard_map/all_gather | solution.py:93
  2361.1 25.6 reshape.140
  2522.8 20.2 all-reduce.14
  2545.9 88.2 %all-reduce.35.cloned.1.call-done = (bf16[3,576,288]{1,2,0:T(8,128)(2,1)}, bf16[288,576]{1,0:T(8,128)(2,1)}, bf16[576,1076]{1,0:T(8,128)(2,1)}, bf16[1076,576]{0,1:T(8,128)(2,1)}) async-done(((bf16[3,576,288]{1,2,0:T(8,128)(2,1)}, bf16[288,576]{1,0:T(8,128)(2,1)}, bf16[576,1076]{1,0:T(8,128)(2,1)}, bf16[1076,576]{0,1:T(8,128)(2,1)}), (bf16[3,576,288]{1,2,0:T(8,128)(2,1)}, bf16[288,576]{1,0:T(8,128)(2,1)}, ...) | async-done | bytes 3806224 | tf_op jit(solution)/shard_map/psum | solution.py:244
  2642.4 229.9 %all-reduce.33.cloned.1.call-done = (bf16[5832,576]{0,1:T(8,128)(2,1)}, bf16[5832,576]{0,1:T(8,128)(2,1)}) async-done(((bf16[5832,576]{0,1:T(8,128)(2,1)}, bf16[5832,576]{0,1:T(8,128)(2,1)}), (bf16[5832,576]{0,1:T(8,128)(2,1)}, bf16[5832,576]{0,1:T(8,128)(2,1)})) %all-reduce.33.cloned.1.call-update) | async-done | bytes 13436944
  2896.6 58.4 %all-reduce.8 = (f32[576]{0:T(1024)}, f32[576]{0:T(1024)}, f32[576]{0:T(1024)}, f32[576]{0:T(1024)}) all-reduce(f32[576]{0:T(1024)S(1)} %broadcast_multiply_fusion.9, f32[576]{0:T(1024)S(1)} %broadcast_multiply_fusion.8, f32[576]{0:T(1024)S(1)} %get-tuple-element.242, ...), channel_id=1, replica_groups=mesh['dp'=4,'row'=4,'col'=2] {'dp','row'}, use_global_device_ids=true, to_apply=%region_40.41 | all-reduce | flops 2304 | bytes 18432 | tf_op jit(solution)/shard_map/psum | solution.py:257
  (305 shorter events, 693.9 us)
Async XLA Ops:
  7.2 915.0 %copy-start = (bf16[576,1076]{1,0:T(8,128)(2,1)S(1)}, bf16[576,1076]{1,0:T(8,128)(2,1)}, u32[]{:S(2)}) copy-start(bf16[576,1076]{1,0:T(8,128)(2,1)} %param.29) | copy-start | bytes 3718660
  7.2 407.9 %all-reduce.25.cloned.1.call-start = ((), (), s32[]{:S(2)}) async-start(), calls=%async_computation.4 | async-start | bytes 20348928
  23.3 3.9 collective-permute-start
  31.4 78.9 %collective-permute-start.1 = (bf16[2,1458,576]{1,2,0:T(8,128)(2,1)}, bf16[2,1458,576]{1,2,0:T(8,128)(2,1)}, u32[]{:S(2)}, u32[]{:S(2)}) collective-permute-start(bf16[2,1458,576]{1,2,0:T(8,128)(2,1)} %get-tuple-element.236), channel_id=1, source_target_pairs={{0,4},{2,6},{4,0},{6,2},{1,5},{3,7},{5,1},{7,3},{8,12},{10,14},{12... | collective-permute-start | bytes 10077704 | tf_op jit(solution)/shard_map/ppermute | solution.py:23
  178.2 373.0 %all-gather.9.cloned.1.call-start = ((), (), s32[]{:S(2)}) async-start(), calls=%async_computation | async-start | bytes 5087232 | tf_op jit(solution)/shard_map/all_gather | solution.py:93
  503.4 261.8 %all-reduce.27.cloned.1.call-start = ((), (), s32[]{:S(2)}) async-start(), calls=%async_computation.5 | async-start | bytes 13565952
  572.5 928.8 %all-reduce.37.cloned.1.call-start = ((), (), s32[]{:S(2)}) async-start(), calls=%async_computation.10 | async-start | bytes 50872320
  576.0 5.2 collective-permute-start.4
  586.9 203.3 %collective-permute-start.5 = (bf16[2,1458,576]{1,2,0:T(8,128)(2,1)}, bf16[2,1458,576]{1,2,0:T(8,128)(2,1)}, u32[]{:S(2)}, u32[]{:S(2)}) collective-permute-start(bf16[2,1458,576]{1,2,0:T(8,128)(2,1)} %get-tuple-element.230), channel_id=1, source_target_pairs={{0,4},{2,6},{4,0},{6,2},{1,5},{3,7},{5,1},{7,3},{8,12},{10,14},{12... | collective-permute-start | bytes 10077704 | tf_op jit(solution)/shard_map/ppermute | solution.py:23
  781.7 3.8 collective-permute-start.2
  789.7 78.9 %collective-permute-start.3 = (bf16[2,1458,576]{1,2,0:T(8,128)(2,1)}, bf16[2,1458,576]{1,2,0:T(8,128)(2,1)}, u32[]{:S(2)}, u32[]{:S(2)}) collective-permute-start(bf16[2,1458,576]{1,2,0:T(8,128)(2,1)} %get-tuple-element.234), channel_id=1, source_target_pairs={{0,4},{2,6},{4,0},{6,2},{1,5},{3,7},{5,1},{7,3},{8,12},{10,14},{12... | collective-permute-start | bytes 10077704 | tf_op jit(solution)/shard_map/ppermute | solution.py:23
  938.3 563.0 %copy-start.32 = (f32[1076]{0:T(1024)S(1)}, f32[1076]{0:T(1024)}, u32[]{:S(2)}) copy-start(f32[1076]{0:T(1024)} %param.30) | copy-start | bytes 12916
  938.3 738.0 %all-gather.13.cloned.1.call-start = ((), (), s32[]{:S(2)}) async-start(), calls=%async_computation.2 | async-start | bytes 19077120 | tf_op jit(solution)/shard_map/all_gather | solution.py:93
  1521.7 371.8 %all-reduce.29.cloned.1.call-start = ((), (), s32[]{:S(2)}) async-start(), calls=%async_computation.6 | async-start | bytes 13565952
  1765.8 385.6 %all-reduce.31.cloned.1.call-start = ((), (), s32[]{:S(2)}) async-start(), calls=%async_computation.7 | async-start | bytes 6782976
  1913.3 3.8 collective-permute-start.6
  1918.3 78.6 %collective-permute-start.7 = (bf16[2,1458,576]{1,2,0:T(8,128)(2,1)S(1)}, bf16[2,1458,576]{1,2,0:T(8,128)(2,1)S(1)}, u32[]{:S(2)}, u32[]{:S(2)}) collective-permute-start(bf16[2,1458,576]{1,2,0:T(8,128)(2,1)S(1)} %get-tuple-element.228), channel_id=1, source_target_pairs={{0,4},{2,6},{4,0},{6,2},{1,5},{3,7},{5,1},{7,3},{8,12},{10,14},{12... | collective-permute-start | bytes 10077704 | tf_op jit(solution)/shard_map/ppermute | solution.py:23
  2060.7 252.0 %all-gather.11.cloned.1.call-start = ((), (), s32[]{:S(2)}) async-start(), calls=%async_computation.1 | async-start | bytes 19077120 | tf_op jit(solution)/shard_map/all_gather | solution.py:93
  2061.5 377.5 %all-gather.15.cloned.1.call-start = ((), (), s32[]{:S(2)}) async-start(), calls=%async_computation.3 | async-start | bytes 15261696 | tf_op jit(solution)/shard_map/all_gather | solution.py:93
  2312.7 321.4 %all-reduce.35.cloned.1.call-start = ((), (), s32[]{:S(2)}) async-start(), calls=%async_computation.9 | async-start | bytes 8257536 | tf_op jit(solution)/shard_map/psum | solution.py:244
  2480.6 391.7 %all-reduce.33.cloned.1.call-start = ((), (), s32[]{:S(2)}) async-start(), calls=%async_computation.8 | async-start | bytes 27131904
  2639.0 233.3 %copy-start.22 = (f32[1458]{0:T(1024)S(1)}, f32[1458]{0:T(1024)}, u32[]{:S(2)}) copy-start(f32[1458]{0:T(1024)} %copy-done.21) | copy-start | bytes 17500
  2639.0 233.3 %copy-start.25 = (f32[576]{0:T(1024)S(1)}, f32[576]{0:T(1024)}, u32[]{:S(2)}) copy-start(f32[576]{0:T(1024)} %param.25) | copy-start | bytes 6916
  2642.4 243.3 %copy-start.34 = (f32[576]{0:T(1024)S(1)}, f32[576]{0:T(1024)}, u32[]{:S(2)}) copy-start(f32[576]{0:T(1024)} %param.32) | copy-start | bytes 6916
  (51 other events, 1191.4 us)
Sparse Core Ops, SparseCore 0:
  178.3 236.7 all-reduce.24
  503.5 47.6 all-gather.8
  572.6 192.5 all-reduce.26
  938.4 562.7 all-reduce.36
  1521.8 154.4 all-gather.12
  1765.9 127.5 all-reduce.28
  2060.9 90.4 all-reduce.30
  2152.9 153.9 all-gather.10
  2312.8 126.1 all-gather.14
  2480.7 153.3 all-reduce.34
  2636.7 235.4 all-reduce.32
